TPU v7x, 512 devices: a whole 4x8x8 slice. The times are simulated.
512 devices in a mesh: wide: 64 (over y, z), narrow: 8 (over x, core).
Axes of the slice: x: 4, y: 8, z: 8, core: 2. Of those that a mesh axis runs over, the one named last changes fastest.
Arguments:
- hidden: bfloat16 [16384, 1536], P('wide', 'narrow'), may hold values from -6 to 6
- start_state: bfloat16 [1024, 24, 64, 128], P('wide', 'narrow'), may hold values from -0.59765625 to 0.59765625
- tail_inner: bfloat16 [1024, 3, 1536], P('wide', None, 'narrow'), may hold values from -6 to 6
- tail_shared: bfloat16 [1024, 3, 256], P('wide'), may hold values from -6 to 6
- input_gain: float32 [1536], replicated, may hold values from 0.5 to 1.5
- w_gate_inner: bfloat16 [1536, 3072], P(None, 'narrow'), may hold values from -0.15625 to 0.15625
- w_shared: bfloat16 [1536, 256], P(None, 'narrow'), may hold values from -0.15625 to 0.15625
- w_step: bfloat16 [1536, 24], P(None, 'narrow'), may hold values from -0.15625 to 0.15625
- step_bias: float32 [24], P('narrow'), may hold values from -4 to -1
- decay_log: float32 [24], P('narrow'), may hold values from 0 to 2.5
- conv_inner: bfloat16 [4, 1536], P(None, 'narrow'), may hold values from -3 to 3
- conv_inner_bias: float32 [1536], P('narrow'), may hold values from -1.5 to 1.5
- conv_shared: bfloat16 [4, 256], replicated, may hold values from -3 to 3
- conv_shared_bias: float32 [256], replicated, may hold values from -1.5 to 1.5
- skip_gain: float32 [24], P('narrow'), may hold values from 0.5 to 1.5
- gated_gain: float32 [1536], P('narrow'), may hold values from 0.5 to 1.5
- w_output: bfloat16 [1536, 1536], P('narrow'), may hold values from -0.15625 to 0.15625
- next_gain: float32 [1536], replicated, may hold values from 0.5 to 1.5
- w_next: bfloat16 [1536, 3224], P(None, 'narrow'), may hold values from -0.15625 to 0.15625
- dealing: int32 [1024], replicated, may hold values from 0 to 1023, as said below
- accepted: int32 [1024], replicated, may hold values from 0 to 16
- owners: int32 [1024], replicated, may hold values from 0 to 63, as said below
Outputs:
- new_hidden: bfloat16 [16384, 1536], P('wide', 'narrow')
- next_input: bfloat16 [16384, 3224], P('wide', 'narrow')
- kept_state: bfloat16 [1024, 24, 64, 128], P('wide', 'narrow')
- kept_tail_inner: bfloat16 [1024, 3, 1536], P('wide', None, 'narrow')
- kept_tail_shared: bfloat16 [1024, 3, 256], P('wide')
Inputs may be any that keep to these rules, and one draw needn't show every extreme that they name: `dealing`: a permutation of the 1024 requests; slot j lies on index j // 16 of wide. Each owner keeps exactly 16 requests, and the requests of the slots of one index of wide have different owners.
All inputs are finite; a program needn't handle non-finite values.
Results may differ from a plain program's by a relative error of at most 0.02.
Values may be sent and summed in bfloat16 or wider, within the bound.
A program may use at most 64 MiB of HBM per device.

v0:
```python
import jax
import jax.numpy as jnp
from jax import lax
from jax.sharding import PartitionSpec as P

EPSILON = 1e-05
HIGHEST = lax.Precision.HIGHEST


def root_norm(values, gain):
    values = values.astype(jnp.float32)
    factor = lax.rsqrt(jnp.mean(values * values, axis=-1, keepdims=True) + EPSILON)
    return (values * factor * gain).astype(jnp.bfloat16)


def causal_filter(tail, fresh, weight, offset):
    extended = jnp.concatenate([tail, fresh], axis=1)
    length = fresh.shape[1]
    summed = jnp.zeros(fresh.shape, jnp.float32) + offset
    for place in range(weight.shape[0]):
        summed = summed + extended[:, place : place + length].astype(jnp.float32) * weight[
            place
        ].astype(jnp.float32)
    return (jax.nn.silu(summed), extended)


def pick_rows(extended, accepted_now, count):
    length = extended.shape[1]
    wanted = accepted_now[:, None] + jnp.arange(count, dtype=jnp.int32)[None, :]
    onehot = (wanted[:, :, None] == jnp.arange(length, dtype=jnp.int32)[None, None, :]).astype(
        jnp.float32
    )
    return jnp.einsum(
        "rqe,rec->rqc", onehot, extended.astype(jnp.float32), precision=HIGHEST
    ).astype(jnp.bfloat16)


def state_block(
    inner, shared, step_raw, step_bias, decay_log, skip_gain, start_state, accepted_now
):
    states = shared.shape[-1] // 2
    b_part = shared[..., :states]
    c_part = shared[..., states:]
    length = inner.shape[1]
    steps_now = jax.nn.softplus(step_raw.astype(jnp.float32) + step_bias)
    log_decay = steps_now * -jnp.exp(decay_log)
    cumul = jnp.cumsum(log_decay, axis=1)
    prefix = jnp.concatenate([jnp.zeros_like(cumul[:, :1]), cumul], axis=1)
    places = jnp.arange(length, dtype=jnp.int32)
    lower = (places[:, None] >= places[None, :])[None, :, :, None]
    spread = cumul[:, :, None, :] - cumul[:, None, :, :]
    weights = (
        jnp.where(lower, jnp.exp(jnp.where(lower, spread, 0.0)), 0.0) * steps_now[:, None, :, :]
    )
    intersection = jnp.einsum("rtn,rsn->rts", c_part, b_part, precision=HIGHEST)
    mixing = weights * intersection[:, :, :, None]
    state_now = start_state.astype(jnp.float32)
    carried = (
        jnp.einsum("rtn,rhpn->rthp", c_part, state_now, precision=HIGHEST)
        * jnp.exp(cumul)[:, :, :, None]
    )
    direct = jnp.einsum("rtsh,rshp->rthp", mixing, inner, precision=HIGHEST)
    outputs = carried + direct + skip_gain[:, None] * inner
    chosen = (jnp.arange(length + 1, dtype=jnp.int32)[None, :] == accepted_now[:, None]).astype(
        jnp.float32
    )
    ending = jnp.einsum("rk,rkh->rh", chosen, prefix, precision=HIGHEST)
    before = (places[None, :] < accepted_now[:, None])[:, :, None]
    factor = (
        jnp.where(before, jnp.exp(jnp.where(before, ending[:, None, :] - cumul, 0.0)), 0.0)
        * steps_now
    )
    kept = jnp.exp(ending)[:, :, None, None] * state_now + jnp.einsum(
        "rsh,rshp,rsn->rhpn", factor, inner, b_part, precision=HIGHEST
    )
    return (outputs, kept.astype(jnp.bfloat16))


def local(
    hidden,
    start_state,
    tail_inner,
    tail_shared,
    input_gain,
    w_gate_inner,
    w_shared,
    w_step,
    step_bias,
    decay_log,
    conv_inner,
    conv_inner_bias,
    conv_shared,
    conv_shared_bias,
    skip_gain,
    gated_gain,
    w_output,
    next_gain,
    w_next,
    dealing,
    accepted,
    owners,
):
    wide_index = lax.axis_index("wide")
    wide_count = lax.axis_size("wide")
    narrow_count = lax.axis_size("narrow")
    full_rows = lax.all_gather(hidden, "narrow", axis=1, tiled=True)
    normed_in = root_norm(full_rows, input_gain)
    tokens = full_rows.shape[0]
    requests = start_state.shape[0]
    length = tokens // requests
    heads_here = w_step.shape[1]
    head_size = start_state.shape[2]
    block = w_output.shape[0]
    gate_inner = jnp.dot(normed_in, w_gate_inner, preferred_element_type=jnp.float32).astype(
        jnp.bfloat16
    )
    shared_piece = jnp.dot(normed_in, w_shared, preferred_element_type=jnp.float32).astype(
        jnp.bfloat16
    )
    step_raw = jnp.dot(normed_in, w_step, preferred_element_type=jnp.float32).astype(jnp.bfloat16)
    shared_in = lax.all_gather(shared_piece, "narrow", axis=1, tiled=True)
    gate_part = gate_inner[:, :block]
    inner_in = gate_inner[:, block:]
    inner_conv, inner_ext = causal_filter(
        tail_inner, inner_in.reshape(requests, length, block), conv_inner, conv_inner_bias
    )
    shared_conv, shared_ext = causal_filter(
        tail_shared, shared_in.reshape(requests, length, -1), conv_shared, conv_shared_bias
    )
    first_slot = wide_index * requests
    slot_requests = lax.dynamic_slice_in_dim(dealing, first_slot, requests)
    accepted_now = jnp.take(accepted, slot_requests)
    outputs, kept = state_block(
        inner_conv.reshape(requests, length, heads_here, head_size),
        shared_conv,
        step_raw.reshape(requests, length, heads_here),
        step_bias,
        decay_log,
        skip_gain,
        start_state,
        accepted_now,
    )
    gated = outputs.reshape(tokens, block) * jax.nn.silu(gate_part.astype(jnp.float32))
    squares = lax.psum(jnp.sum(gated * gated, axis=1, keepdims=True), "narrow")
    gated_norm = (
        gated * lax.rsqrt(squares / (block * narrow_count) + EPSILON) * gated_gain
    ).astype(jnp.bfloat16)
    partial_sum = jnp.dot(gated_norm, w_output, preferred_element_type=jnp.float32)
    whole_sum = lax.psum(partial_sum.astype(jnp.bfloat16), "narrow").astype(jnp.float32)
    new_full = (full_rows.astype(jnp.float32) + whole_sum).astype(jnp.bfloat16)
    new_part = lax.dynamic_slice_in_dim(
        new_full, lax.axis_index("narrow") * hidden.shape[1], hidden.shape[1], 1
    )
    normed_next = root_norm(new_full, next_gain)
    next_input = jnp.dot(normed_next, w_next, preferred_element_type=jnp.float32).astype(
        jnp.bfloat16
    )
    owner_table = (owners[:, None] == jnp.arange(wide_count, dtype=jnp.int32)[None, :]).astype(
        jnp.int32
    )
    ranking = jnp.sum((jnp.cumsum(owner_table, axis=0) - owner_table) * owner_table, axis=1)
    slot_owner = jnp.take(owners, dealing)
    slot_rank = jnp.take(ranking, dealing)
    local_owner = lax.dynamic_slice_in_dim(slot_owner, first_slot, requests)
    send_table = (jnp.arange(wide_count, dtype=jnp.int32)[:, None] == local_owner[None, :]).astype(
        jnp.bfloat16
    )
    state_bucket = (
        jnp.dot(send_table, kept.reshape(requests, -1), preferred_element_type=jnp.float32)
        .astype(jnp.bfloat16)
        .reshape((wide_count,) + kept.shape[1:])
    )
    inner_edge = pick_rows(inner_ext, accepted_now, tail_inner.shape[1])
    shared_edge = pick_rows(shared_ext, accepted_now, tail_shared.shape[1])
    inner_bucket = jnp.einsum(
        "or,rqc->oqc", send_table, inner_edge, preferred_element_type=jnp.float32
    ).astype(jnp.bfloat16)
    shared_bucket = jnp.einsum(
        "or,rqc->oqc", send_table, shared_edge, preferred_element_type=jnp.float32
    ).astype(jnp.bfloat16)
    state_recv, inner_recv, shared_recv = (
        lax.all_to_all(state_bucket, "wide", split_axis=0, concat_axis=0, tiled=True),
        lax.all_to_all(inner_bucket, "wide", split_axis=0, concat_axis=0, tiled=True),
        lax.all_to_all(shared_bucket, "wide", split_axis=0, concat_axis=0, tiled=True),
    )
    senders = jnp.arange(slot_owner.shape[0], dtype=jnp.int32) // requests
    mine = slot_owner == wide_index
    picking = (
        (slot_rank[:, None] == jnp.arange(requests, dtype=jnp.int32)[None, :]) & mine[:, None]
    ).astype(jnp.bfloat16)
    from_sender = (senders[:, None] == jnp.arange(wide_count, dtype=jnp.int32)[None, :]).astype(
        jnp.bfloat16
    )
    selector = jnp.einsum(
        "jk,jw->kw", picking, from_sender, preferred_element_type=jnp.float32
    ).astype(jnp.bfloat16)
    kept_state = (
        jnp.dot(selector, state_recv.reshape(wide_count, -1), preferred_element_type=jnp.float32)
        .astype(jnp.bfloat16)
        .reshape(start_state.shape)
    )
    kept_tail_inner = jnp.einsum(
        "kw,wqc->kqc", selector, inner_recv, preferred_element_type=jnp.float32
    ).astype(jnp.bfloat16)
    kept_tail_shared = jnp.einsum(
        "kw,wqc->kqc", selector, shared_recv, preferred_element_type=jnp.float32
    ).astype(jnp.bfloat16)
    return (new_part, next_input, kept_state, kept_tail_inner, kept_tail_shared)


def solution(mesh):
    placed = (
        P("wide", "narrow"),
        P("wide", "narrow", None, None),
        P("wide", None, "narrow"),
        P("wide", None, None),
        P(),
        P(None, "narrow"),
        P(None, "narrow"),
        P(None, "narrow"),
        P("narrow"),
        P("narrow"),
        P(None, "narrow"),
        P("narrow"),
        P(),
        P(),
        P("narrow"),
        P("narrow"),
        P("narrow", None),
        P(),
        P(None, "narrow"),
        P(),
        P(),
        P(),
    )
    return jax.shard_map(
        local,
        mesh=mesh,
        in_specs=placed,
        out_specs=(
            P("wide", "narrow"),
            P("wide", "narrow"),
            P("wide", "narrow", None, None),
            P("wide", None, "narrow"),
            P("wide", None, None),
        ),
        check_vma=False,
    )
```

profile of v0, /device:TPU:24, one launch (start us, length us, event | category | flops | bytes accessed | tf_op | source)
XLA Modules:
  0.0 219.7 jit_solution(16669502044702229559)
XLA Ops:
  7.2 0.8 fusion.81
  8.0 0.8 compare_select_fusion.2
  8.8 1.3 gather_fusion
  10.1 0.8 and_select_fusion
  10.9 4.5 %gather_fusion.2 = s32[1024]{0:T(1024)S(1)} fusion(s32[1024]{0:T(1024)S(1)} %copy-done.1, s32[1024]{0:T(1024)S(1)} %fusion.81), kind=kCustom, calls=%fused_computation.1.clone | custom fusion | bytes 12288 | tf_op jit(solution)/shard_map/jit(_take)/gather | solution.py:162
  15.4 0.6 broadcast_compare_fusion
  16.2 13.7 %all_gather.6 = bf16[256,1536]{0,1:T(8,128)(2,1)S(1)} all-gather(bf16[256,192]{0,1:T(8,128)(2,1)S(1)} %copy-done.7), channel_id=1, replica_groups=mesh['wide'=64,'narrow'=8] {'narrow'}, dimensions={1}, use_global_device_ids=true | all-gather | bytes 884736 | tf_op jit(solution)/shard_map/all_gather | solution.py:106
  29.9 0.3 copy.79
  30.2 0.2 fusion.6
  30.5 1.9 convolution_convert_fusion.4
  32.6 0.5 copy-done.6
  33.1 0.2 convolution_convert_fusion.8
  33.4 0.3 convolution_convert_fusion.6
  33.7 0.7 copy.98
  34.4 16.6 %all-to-all-start.1 = ((bf16[64,3,192]{2,1,0:T(4,128)(2,1)}), bf16[64,3,192]{2,1,0:T(4,128)(2,1)}, u32[]{:S(2)}, u32[]{:S(2)}) async-start(bf16[64,3,192]{2,1,0:T(4,128)(2,1)} %copy.98), calls=%async_computation.1 | async-start | bytes 262144 | tf_op jit(solution)/shard_map/all_to_all | solution.py:183
  51.2 0.6 slice_convert_fusion.7
  51.9 0.4 fusion.15
  52.3 0.4 convolution_convert_fusion.11
  52.8 0.1 broadcast_multiply_fusion.1
  52.9 0.2 copy.82
  53.1 0.7 fusion.90
  53.8 0.2 copy.94
  54.4 0.8 copy.95
  55.2 12.7 %all_gather.7 = bf16[256,256]{0,1:T(8,128)(2,1)S(1)} all-gather(bf16[256,32]{0,1:T(8,128)(2,1)S(1)} %convolution_convert_fusion.11), channel_id=1, replica_groups=mesh['wide'=64,'narrow'=8] {'narrow'}, dimensions={1}, use_global_device_ids=true | all-gather | bytes 147456 | tf_op jit(solution)/shard_map/all_gather | solution.py:121
  68.0 0.2 convolution_convert_fusion.7
  68.3 0.3 convolution_convert_fusion.5
  68.6 0.1 copy-done.5
  68.7 0.7 copy.101
  69.4 0.9 divide_multiply_fusion
  70.4 1.1 reshape.238
  71.5 2.2 %broadcast_multiply_fusion = f32[16,16,3,64]{3,2,1,0:T(4,128)} fusion(f32[16,16,3,64]{3,2,1,0:T(4,128)S(1)} %reshape.238, f32[16,16,3]{2,1,0:T(8,128)} %copy.95), kind=kLoop, calls=%fused_computation.72 | loop fusion | flops 49152 | bytes 396288 | tf_op jit(solution)/shard_map/rsh,rshp,rsn->rhpn/dot_general | solution.py:73
  73.7 1.5 divide_multiply_fusion.1
  75.2 12.7 %all-to-all-start.2 = ((bf16[64,3,256]{2,1,0:T(4,128)(2,1)}), bf16[64,3,256]{2,1,0:T(4,128)(2,1)S(1)}, u32[]{:S(2)}, u32[]{:S(2)}) async-start(bf16[64,3,256]{2,1,0:T(4,128)(2,1)} %copy.101), calls=%async_computation.2 | async-start | bytes 262144 | tf_op jit(solution)/shard_map/all_to_all | solution.py:184
  87.9 3.8 %add_convert_fusion = bf16[16,3,64,128]{3,2,1,0:T(8,128)(2,1)S(1)} fusion(bf16[16,3,64,128]{3,2,1,0:T(8,128)(2,1)S(1)} %copy-done.2, f32[16,3]{1,0:T(8,128)S(1)} %copy.93, f32[16,16,3,64]{3,2,1,0:T(4,128)} %broadcast_multiply_fusion, f32[16,16,256]{2,1,0:T(8,128)S(1)} %divide_multiply_fusion.1), kind=kOutput, calls=%fused_computation.21 | convolution fusion | flops 77070336 | bytes 1908736 | tf_op jit(solution)/shard_map/rsh,rshp,rsn->rhpn/dot_general | solution.py:73
  91.7 1.8 fusion.2
  93.5 2.5 %copy.114 = bf16[8,8,192,128]{3,2,1,0:T(8,128)(2,1)} copy(bf16[8,8,192,128]{3,1,2,0:T(8,128)(2,1)S(1)} %fusion.2) | data formatting | bytes 6291456
  96.0 2.8 %all-to-all-done.2 = bf16[64,3,256]{2,1,0:T(4,128)(2,1)S(1)} async-done(((bf16[64,3,256]{2,1,0:T(4,128)(2,1)}), bf16[64,3,256]{2,1,0:T(4,128)(2,1)S(1)}, u32[]{:S(2)}, u32[]{:S(2)}) %all-to-all-start.2) | async-done | bytes 98336 | tf_op jit(solution)/shard_map/all_to_all | solution.py:184
  98.8 10.3 %all-to-all-start = ((bf16[64,3,64,128]{3,2,1,0:T(8,128)(2,1)}), bf16[64,3,64,128]{3,2,1,0:T(8,128)(2,1)}, u32[]{:S(2)}, u32[]{:S(2)}) async-start(bf16[64,3,64,128]{3,2,1,0:T(8,128)(2,1)} %bitcast.87), calls=%async_computation | async-start | bytes 6291456 | tf_op jit(solution)/shard_map/all_to_all | solution.py:182
  109.1 0.6 copy.87
  109.7 0.8 copy.85
  110.5 0.2 copy.83
  110.8 0.3 fusion.59
  111.1 1.7 convolution_multiply_fusion
  112.9 0.6 fusion.14
  113.5 0.2 copy.90
  113.7 0.3 reshape.239
  114.0 1.1 multiply_reduce_fusion
  115.1 14.5 %psum.14 = f32[256,1]{0,1:T(1,128)S(1)} all-reduce(f32[256,1]{0,1:T(1,128)S(1)} %bitcast.96), channel_id=1, replica_groups=mesh['wide'=64,'narrow'=8] {'narrow'}, use_global_device_ids=true, to_apply=%region_3.4 | all-reduce | flops 256 | bytes 2048 | tf_op jit(solution)/shard_map/psum | solution.py:144
  129.7 2.4 %convolution_convert_fusion.2 = bf16[256,1536]{1,0:T(8,128)(2,1)} fusion(bf16[192,1536]{1,0:T(8,128)(2,1)} %param.40, f32[192]{0:T(256)S(1)} %copy-done.24, f32[256]{0:T(256)S(1)} %bitcast.105, f32[256,192]{1,0:T(8,128)S(1)} %reshape.239, bf16[256,384]{1,0:T(8,128)(2,1)} %copy-done.6), kind=kOutput, calls=%fused_computation.7 | convolution fusion | flops 151830528 | bytes 1705728 | tf_op jit(solution)/shard_map/dot_general | solution.py:148
  132.2 18.0 %reduce-window.6 = s32[64,8,128]{2,1,0:T(8,128)S(1)} reduce-window(s32[64,8,128]{2,1,0:T(8,128)S(1)} %fusion.41, s32[]{:T(128)} %constant.71.clone.1), window={size=1x1x128 pad=0_0x0_0x127_0}, to_apply=%region_6.7 | reduce-window | flops 8323072 | bytes 524292 | tf_op jit(solution)/shard_map/reduce-window
  150.2 0.1 slice.102
  150.3 0.1 copy.91
  150.6 0.1 broadcast_add_fusion
  150.8 4.5 %gather_fusion.1 = s32[1024]{0:T(1024)S(1)} fusion(s32[1024]{0:T(1024)S(1)} %fusion.37, s32[1024]{0:T(1024)S(1)} %fusion.81), kind=kCustom, calls=%fused_computation.clone | custom fusion | bytes 12288 | tf_op jit(solution)/shard_map/jit(_take)/gather | solution.py:163
  155.4 0.8 convolution_convert_fusion.12
  156.2 1.7 convolution_convert_fusion.10
  157.8 0.7 convolution_convert_fusion.9
  158.6 45.9 %all-reduce.3.cloned.1.call-done = bf16[256,1536]{1,0:T(8,128)(2,1)} async-done(((bf16[256,1536]{1,0:T(8,128)(2,1)}), bf16[256,1536]{1,0:T(8,128)(2,1)}) %all-reduce.3.cloned.1.call-update) | async-done | bytes 786448 | tf_op jit(solution)/shard_map/psum | solution.py:149
  204.5 1.5 fusion.3
  206.0 0.1 constant_dynamic-slice_fusion
  206.1 0.7 copy.103
  206.8 1.3 convolution_convert_fusion.3
  208.2 3.7 %fusion.10 = bf16[2,8,192,128]{3,1,2,0:T(8,128)(2,1)S(1)} fusion(bf16[16,64]{1,0:T(8,128)(2,1)S(1)} %convolution_convert_fusion.12, bf16[8,8,192,128]{3,2,1,0:T(8,128)(2,1)} %bitcast.34), kind=kOutput, calls=%fused_computation.22 | convolution fusion | flops 50724864 | bytes 3934208 | tf_op jit(solution)/shard_map/dot_general | solution.py:198
  211.8 1.0 copy.116
  (85 shorter events, 1.5 us)
Async XLA Ops:
  7.2 199.7 %copy-start = (bf16[1536,403]{0,1:T(8,128)(2,1)S(1)}, bf16[1536,403]{0,1:T(8,128)(2,1)}, u32[]{:S(2)}) copy-start(bf16[1536,403]{0,1:T(8,128)(2,1)} %param.42) | copy-start | bytes 3714052
  7.2 3.7 %copy-start.1 = (s32[1024]{0:T(1024)S(1)}, s32[1024]{0:T(1024)}, u32[]{:S(2)}) copy-start(s32[1024]{0:T(1024)} %param.45) | copy-start | bytes 12292
  10.9 4.6 %copy-start.12 = (s32[1024]{0:T(1024)S(1)}, s32[1024]{0:T(1024)}, u32[]{:S(2)}) copy-start(s32[1024]{0:T(1024)} %param.43) | copy-start | bytes 12292
  10.9 5.3 %copy-start.10 = (bf16[16,3,192]{2,0,1:T(8,128)(2,1)S(1)}, bf16[16,3,192]{2,0,1:T(8,128)(2,1)}, u32[]{:S(2)}) copy-start(bf16[16,3,192]{2,0,1:T(8,128)(2,1)} %param.26) | copy-start | bytes 55300
  10.9 5.3 %copy-start.7 = (bf16[256,192]{0,1:T(8,128)(2,1)S(1)}, bf16[256,192]{0,1:T(8,128)(2,1)}, u32[]{:S(2)}) copy-start(bf16[256,192]{0,1:T(8,128)(2,1)} %param.24) | copy-start | bytes 294916
  16.1 52.2 %copy-start.15 = (s32[16]{0:T(128)}, s32[16]{0:T(128)S(1)}, u32[]{:S(2)}) copy-start(s32[16]{0:T(128)S(1)} %dynamic_slice.10) | copy-start | bytes 196
  16.2 14.3 %copy-start.22 = (f32[1536]{0:T(1024)S(1)}, f32[1536]{0:T(1024)}, u32[]{:S(2)}) copy-start(f32[1536]{0:T(1024)} %param.28) | copy-start | bytes 18436
  30.5 20.7 %copy-start.25 = (f32[3]{0:T(128)S(1)}, f32[3]{0:T(128)}, u32[]{:S(2)}) copy-start(f32[3]{0:T(128)} %param.33) | copy-start | bytes 40
  30.5 20.7 %copy-start.13 = (bf16[4,192]{1,0:T(4,128)(2,1)S(1)}, bf16[4,192]{1,0:T(4,128)(2,1)}, u32[]{:S(2)}) copy-start(bf16[4,192]{1,0:T(4,128)(2,1)} %param.34) | copy-start | bytes 4612
  30.5 20.7 %copy-start.14 = (bf16[4,256]{1,0:T(4,128)(2,1)S(1)}, bf16[4,256]{1,0:T(4,128)(2,1)}, u32[]{:S(2)}) copy-start(bf16[4,256]{1,0:T(4,128)(2,1)} %param.36) | copy-start | bytes 6148
  30.5 21.4 %copy-start.11 = (bf16[16,3,256]{2,0,1:T(8,128)(2,1)S(1)}, bf16[16,3,256]{2,0,1:T(8,128)(2,1)}, u32[]{:S(2)}) copy-start(bf16[16,3,256]{2,0,1:T(8,128)(2,1)} %param.27) | copy-start | bytes 73732
  30.5 21.4 %copy-start.21 = (bf16[1536,3]{0,1:T(4,128)(2,1)S(1)}, bf16[1536,3]{0,1:T(4,128)(2,1)}, u32[]{:S(2)}) copy-start(bf16[1536,3]{0,1:T(4,128)(2,1)} %param.31) | copy-start | bytes 27652
  32.5 0.7 copy-start.6
  32.5 19.8 %copy-start.20 = (bf16[1536,32]{0,1:T(8,128)(2,1)S(1)}, bf16[1536,32]{0,1:T(8,128)(2,1)}, u32[]{:S(2)}) copy-start(bf16[1536,32]{0,1:T(8,128)(2,1)} %param.30) | copy-start | bytes 294916
  34.4 40.8 %all-to-all-start.1 = ((bf16[64,3,192]{2,1,0:T(4,128)(2,1)}), bf16[64,3,192]{2,1,0:T(4,128)(2,1)}, u32[]{:S(2)}, u32[]{:S(2)}) async-start(bf16[64,3,192]{2,1,0:T(4,128)(2,1)} %copy.98), calls=%async_computation.1 | async-start | bytes 262144 | tf_op jit(solution)/shard_map/all_to_all | solution.py:183
  51.0 1.8 copy-start.19
  52.3 17.1 %copy-start.17 = (f32[192]{0:T(256)S(1)}, f32[192]{0:T(256)}, u32[]{:S(2)}) copy-start(f32[192]{0:T(256)} %param.35) | copy-start | bytes 2308
  68.0 0.7 copy-start.5
  69.4 18.5 %copy-start.2 = (bf16[16,3,64,128]{3,2,1,0:T(8,128)(2,1)S(1)}, bf16[16,3,64,128]{3,2,1,0:T(8,128)(2,1)}, u32[]{:S(2)}) copy-start(bf16[16,3,64,128]{3,2,1,0:T(8,128)(2,1)} %param.25) | copy-start | bytes 2359300
  71.5 2.2 %copy-start.3 = (f32[16,16,3,64]{3,2,1,0:T(4,128)}, f32[16,16,3,64]{3,2,1,0:T(4,128)S(1)}, u32[]{:S(2)}) copy-start(f32[16,16,3,64]{3,2,1,0:T(4,128)S(1)} %reshape.238) | copy-start | bytes 589828
  75.2 23.6 %all-to-all-start.2 = ((bf16[64,3,256]{2,1,0:T(4,128)(2,1)}), bf16[64,3,256]{2,1,0:T(4,128)(2,1)S(1)}, u32[]{:S(2)}, u32[]{:S(2)}) async-start(bf16[64,3,256]{2,1,0:T(4,128)(2,1)} %copy.101), calls=%async_computation.2 | async-start | bytes 262144 | tf_op jit(solution)/shard_map/all_to_all | solution.py:184
  98.8 109.4 %all-to-all-start = ((bf16[64,3,64,128]{3,2,1,0:T(8,128)(2,1)}), bf16[64,3,64,128]{3,2,1,0:T(8,128)(2,1)}, u32[]{:S(2)}, u32[]{:S(2)}) async-start(bf16[64,3,64,128]{3,2,1,0:T(8,128)(2,1)} %bitcast.87), calls=%async_computation | async-start | bytes 6291456 | tf_op jit(solution)/shard_map/all_to_all | solution.py:182
  109.0 3.8 %copy-start.26 = (f32[3]{0:T(128)S(1)}, f32[3]{0:T(128)}, u32[]{:S(2)}) copy-start(f32[3]{0:T(128)} %param.38) | copy-start | bytes 40
  109.1 95.4 %all-reduce.3.cloned.1.call-start = ((), (), s32[]{:S(2)}) async-start(), calls=%async_computation.3 | async-start | bytes 1572864 | tf_op jit(solution)/shard_map/psum | solution.py:149
  110.7 2.1 copy-start.4
  110.7 2.1 copy-start.8
  110.7 2.1 copy-start.9
  112.9 16.8 %copy-start.24 = (f32[192]{0:T(256)S(1)}, f32[192]{0:T(256)}, u32[]{:S(2)}) copy-start(f32[192]{0:T(256)} %param.39) | copy-start | bytes 2308
  150.8 4.6 %copy-start.16 = (pred[1024]{0:T(1024)(128)(4,1)S(1)}, pred[1024]{0:T(1024)(128)(4,1)}, u32[]{:S(2)}) copy-start(pred[1024]{0:T(1024)(128)(4,1)} %get-tuple-element.28) | copy-start | bytes 3076
  150.8 4.6 %copy-start.18 = (pred[1024]{0:T(1024)(128)(4,1)S(1)}, pred[1024]{0:T(1024)(128)(4,1)}, u32[]{:S(2)}) copy-start(pred[1024]{0:T(1024)(128)(4,1)} %get-tuple-element.26) | copy-start | bytes 3076
  156.2 50.7 %copy-start.23 = (f32[1536]{0:T(1024)S(1)}, f32[1536]{0:T(1024)}, u32[]{:S(2)}) copy-start(f32[1536]{0:T(1024)} %param.41) | copy-start | bytes 18436
Sparse Core Ops, SparseCore 0:
  132.2 72.1 all-reduce.2
where the time goes:
time: 220 us
  waiting for transfers between devices  48.7 us (22%)
  blocking collectives  41 us (19%)
  starting transfers between devices  39.6 us (18%)
  other arithmetic  30.4 us (14%)
  local copies, waits for them, and re-layouts  22.8 us (10%)
  matrix products  22.6 us (10%)
  between operations  14.6 us (7%)
    psum x1, waiting for transfers between devices, local(): lax.psum(partial_sum.astype(jnp.bfloat16), 'narrow').astype(jnp.float32)  45.9 us
    another operation x3, other arithmetic  18.2 us
    all_to_all x1, starting transfers between devices, local(): lax.all_to_all(inner_bucket, 'wide', split_axis=0, concat_axis=0, tiled=T...  16.6 us
    psum x1, blocking collectives, local(): squares = lax.psum(jnp.sum(gated * gated, axis=1, keepdims=True), 'narrow')  14.5 us
    all_gather x1, blocking collectives, local(): full_rows = lax.all_gather(hidden, 'narrow', axis=1, tiled=True)  13.7 us
    all_gather x1, blocking collectives, local(): shared_in = lax.all_gather(shared_piece, 'narrow', axis=1, tiled=True)  12.7 us
    all_to_all x1, starting transfers between devices, local(): lax.all_to_all(shared_bucket, 'wide', split_axis=0, concat_axis=0, tiled=...  12.7 us
    all_to_all x1, starting transfers between devices, local(): lax.all_to_all(state_bucket, 'wide', split_axis=0, concat_axis=0, tiled=T...  10.3 us
  transfers between devices with their start and end apart: 4, of which 2 were waited for; matrix products, arithmetic and copies ran while one was open for 26% of the time, Pallas kernels for 0%

commit v1 on v0

--- a/solution.py
+++ b/solution.py
@@ -5,6 +5,32 @@
 
 EPSILON = 1e-05
 HIGHEST = lax.Precision.HIGHEST
+
+
+def set_put(inputs):
+    field_out = lax.psum(1, "narrow")
+    val2 = lax.axis_index("narrow")
+    frame_out, t_next, heard = (field_out, val2, inputs.shape[1])
+    z2 = jnp.zeros(
+        [q * frame_out if jj == 1 else q for jj, q in enumerate(inputs.shape)], inputs.dtype
+    )
+    piece_now = lax.dynamic_update_slice_in_dim(z2, inputs, t_next * heard, axis=1)
+    taken_in = row_out = inputs
+    for b in range(1, frame_out // 2 + 1):
+        taken_in = lax.ppermute(
+            taken_in, "narrow", [(jj, (jj + 1) % frame_out) for jj in range(frame_out)]
+        )
+        piece_now = lax.dynamic_update_slice_in_dim(
+            piece_now, taken_in, (t_next - b) % frame_out * heard, axis=1
+        )
+        if 2 * b < frame_out:
+            row_out = lax.ppermute(
+                row_out, "narrow", [(jj, (jj - 1) % frame_out) for jj in range(frame_out)]
+            )
+            piece_now = lax.dynamic_update_slice_in_dim(
+                piece_now, row_out, (t_next + b) % frame_out * heard, axis=1
+            )
+    return piece_now
 
 
 def root_norm(values, gain):
@@ -103,7 +129,7 @@
     wide_index = lax.axis_index("wide")
     wide_count = lax.axis_size("wide")
     narrow_count = lax.axis_size("narrow")
-    full_rows = lax.all_gather(hidden, "narrow", axis=1, tiled=True)
+    full_rows = set_put(hidden)
     normed_in = root_norm(full_rows, input_gain)
     tokens = full_rows.shape[0]
     requests = start_state.shape[0]

time: 220 us -> 266 us (1.21)
  the two profiles are of different devices: /device:TPU:24 before, /device:TPU:8 now
where the time goes in v1:
time: 266 us; the launch traced here: 264 us
  waiting for transfers between devices  83 us (31%)
  other arithmetic  42.9 us (16%)
  starting transfers between devices  40.7 us (15%)
  local copies, waits for them, and re-layouts  34.1 us (13%)
  blocking collectives  26.2 us (10%)
  matrix products  22.5 us (8%)
  between operations  14.9 us (6%)
    psum x1, waiting for transfers between devices, local(): lax.psum(partial_sum.astype(jnp.bfloat16), 'narrow').astype(jnp.float32)  68.5 us
    another operation x3, other arithmetic  31 us
    all_to_all x1, starting transfers between devices, local(): lax.all_to_all(inner_bucket, 'wide', split_axis=0, concat_axis=0, tiled=T...  16.8 us
    psum x1, blocking collectives, local(): squares = lax.psum(jnp.sum(gated * gated, axis=1, keepdims=True), 'narrow')  13.4 us
    all_gather x1, blocking collectives, local(): shared_in = lax.all_gather(shared_piece, 'narrow', axis=1, tiled=True)  12.7 us
    all_to_all x1, starting transfers between devices, local(): lax.all_to_all(state_bucket, 'wide', split_axis=0, concat_axis=0, tiled=T...  9.23 us
    ppermute x3, starting transfers between devices, set_put(): lax.ppermute(row_out, 'narrow', [(jj, (jj - 1) % frame_out) for jj in ran...  8.24 us
    all_to_all x1, starting transfers between devices, local(): lax.all_to_all(shared_bucket, 'wide', split_axis=0, concat_axis=0, tiled=...  6.37 us
  transfers between devices with their start and end apart: 11, of which 6 were waited for; matrix products, arithmetic and copies ran while one was open for 32% of the time, Pallas kernels for 0%

profile of v1, /device:TPU:8, one launch (start us, length us, event | category | flops | bytes accessed | tf_op | source)
XLA Modules:
  0.0 264.2 jit_solution(6247746344815310584)
XLA Ops:
  7.2 1.1 copy.85
  8.3 2.2 collective-permute-start.1
  10.5 0.7 fusion.81
  11.2 0.8 compare_select_fusion.2
  12.0 1.3 gather_fusion
  13.3 0.8 and_select_fusion
  14.3 4.5 %gather_fusion.2 = s32[1024]{0:T(1024)S(1)} fusion(s32[1024]{0:T(1024)S(1)} %copy-done.1, s32[1024]{0:T(1024)S(1)} %fusion.81), kind=kCustom, calls=%fused_computation.1.clone | custom fusion | bytes 12288 | tf_op jit(solution)/shard_map/jit(_take)/gather | solution.py:188
  18.8 0.5 broadcast_compare_fusion
  19.4 0.6 slice_convert_fusion.7
  20.0 3.0 %collective-permute-start.3 = (bf16[256,192]{1,0:T(8,128)(2,1)S(1)}, bf16[256,192]{1,0:T(8,128)(2,1)S(1)}, u32[]{:S(2)}, u32[]{:S(2)}) collective-permute-start(bf16[256,192]{1,0:T(8,128)(2,1)S(1)} %collective-permute-done.1), channel_id=1, source_target_pairs={{0,7},{1,0},{2,1},{3,2},{4,3},{5,4},{6,5},{7,6},{8,15},{9,8},{10,9... | collective-permute-start | bytes 294920 | tf_op jit(solution)/shard_map/ppermute | solution.py:27
  23.0 2.0 collective-permute-done.2
  25.1 0.4 collective-permute-done.3
  25.5 3.1 %collective-permute-start.5 = (bf16[256,192]{1,0:T(8,128)(2,1)S(1)}, bf16[256,192]{1,0:T(8,128)(2,1)S(1)}, u32[]{:S(2)}, u32[]{:S(2)}) collective-permute-start(bf16[256,192]{1,0:T(8,128)(2,1)S(1)} %collective-permute-done.3), channel_id=1, source_target_pairs={{0,7},{1,0},{2,1},{3,2},{4,3},{5,4},{6,5},{7,6},{8,15},{9,8},{10,9... | collective-permute-start | bytes 294920 | tf_op jit(solution)/shard_map/ppermute | solution.py:27
  28.6 2.0 collective-permute-done.4
  31.1 1.2 dynamic_update_slice.24
  32.3 1.1 dynamic_update_slice.25
  33.4 1.5 dynamic_update_slice.26
  34.9 0.8 dynamic_update_slice.27
  35.7 1.2 dynamic_update_slice.28
  36.9 1.5 dynamic_update_slice.29
  38.5 1.5 dynamic_update_slice.30
  40.0 1.2 dynamic_update_slice.31
  41.5 0.4 fusion.15
  41.8 0.4 convolution_convert_fusion.11
  42.6 0.7 fusion.90
  43.9 0.8 copy.103
  44.7 12.7 %all_gather.3 = bf16[256,256]{0,1:T(8,128)(2,1)S(1)} all-gather(bf16[256,32]{0,1:T(8,128)(2,1)S(1)} %convolution_convert_fusion.11), channel_id=1, replica_groups=mesh['wide'=64,'narrow'=8] {'narrow'}, dimensions={1}, use_global_device_ids=true | all-gather | bytes 147456 | tf_op jit(solution)/shard_map/all_gather | solution.py:147
  57.8 0.3 convolution_convert_fusion.5
  58.1 0.7 copy.109
  58.8 1.9 convolution_convert_fusion.4
  61.4 0.7 copy.106
  62.1 16.8 %all-to-all-start.1 = ((bf16[64,3,192]{2,1,0:T(4,128)(2,1)}), bf16[64,3,192]{2,1,0:T(4,128)(2,1)}, u32[]{:S(2)}, u32[]{:S(2)}) async-start(bf16[64,3,192]{2,1,0:T(4,128)(2,1)} %copy.106), calls=%async_computation.1 | async-start | bytes 262144 | tf_op jit(solution)/shard_map/all_to_all | solution.py:209
  78.9 0.9 divide_multiply_fusion
  79.9 1.1 reshape.238
  81.0 2.2 broadcast_multiply_fusion
  83.2 1.5 divide_multiply_fusion.1
  84.7 6.4 %all-to-all-done.1 = bf16[64,3,192]{2,1,0:T(4,128)(2,1)} async-done(((bf16[64,3,192]{2,1,0:T(4,128)(2,1)}), bf16[64,3,192]{2,1,0:T(4,128)(2,1)}, u32[]{:S(2)}, u32[]{:S(2)}) %all-to-all-start.1) | async-done | bytes 73760 | tf_op jit(solution)/shard_map/all_to_all | solution.py:209
  91.1 6.4 %all-to-all-start.2 = ((bf16[64,3,256]{2,1,0:T(4,128)(2,1)}), bf16[64,3,256]{2,1,0:T(4,128)(2,1)S(1)}, u32[]{:S(2)}, u32[]{:S(2)}) async-start(bf16[64,3,256]{2,1,0:T(4,128)(2,1)} %copy.109), calls=%async_computation.2 | async-start | bytes 262144 | tf_op jit(solution)/shard_map/all_to_all | solution.py:210
  97.5 3.8 %add_convert_fusion = bf16[16,3,64,128]{3,2,1,0:T(8,128)(2,1)S(1)} fusion(bf16[16,3,64,128]{3,2,1,0:T(8,128)(2,1)S(1)} %copy-done.2, f32[16,3]{1,0:T(8,128)S(1)} %copy.101, f32[16,16,3,64]{3,2,1,0:T(4,128)} %broadcast_multiply_fusion, f32[16,16,256]{2,1,0:T(8,128)S(1)} %divide_multiply_fusion.1), kind=kOutput, calls=%fused_computation.21 | convolution fusion | flops 77070336 | bytes 1908736 | tf_op jit(solution)/shard_map/rsh,rshp,rsn->rhpn/dot_general | solution.py:99
  101.3 1.7 fusion.2
  103.0 2.5 copy.122
  105.5 3.6 %all-to-all-done.2 = bf16[64,3,256]{2,1,0:T(4,128)(2,1)S(1)} async-done(((bf16[64,3,256]{2,1,0:T(4,128)(2,1)}), bf16[64,3,256]{2,1,0:T(4,128)(2,1)S(1)}, u32[]{:S(2)}, u32[]{:S(2)}) %all-to-all-start.2) | async-done | bytes 98336 | tf_op jit(solution)/shard_map/all_to_all | solution.py:210
  109.1 0.6 copy-done.6
  109.8 9.2 %all-to-all-start = ((bf16[64,3,64,128]{3,2,1,0:T(8,128)(2,1)}), bf16[64,3,64,128]{3,2,1,0:T(8,128)(2,1)}, u32[]{:S(2)}, u32[]{:S(2)}) async-start(bf16[64,3,64,128]{3,2,1,0:T(8,128)(2,1)} %bitcast.87), calls=%async_computation | async-start | bytes 6291456 | tf_op jit(solution)/shard_map/all_to_all | solution.py:208
  119.1 0.7 fusion.41
  119.8 30.8 %reduce-window.6 = s32[64,8,128]{2,1,0:T(8,128)S(1)} reduce-window(s32[64,8,128]{2,1,0:T(8,128)} %fusion.41, s32[]{:T(128)} %constant.111.clone.1), window={size=1x1x128 pad=0_0x0_0x127_0}, to_apply=%region_6.7 | reduce-window | flops 8323072 | bytes 524292 | tf_op jit(solution)/shard_map/reduce-window
  150.6 0.8 slice.102
  151.5 1.1 copy.99
  152.9 4.5 %gather_fusion.1 = s32[1024]{0:T(1024)S(1)} fusion(s32[1024]{0:T(1024)S(1)} %fusion.37, s32[1024]{0:T(1024)S(1)} %fusion.81), kind=kCustom, calls=%fused_computation.clone | custom fusion | bytes 12288 | tf_op jit(solution)/shard_map/jit(_take)/gather | solution.py:189
  157.5 0.8 convolution_convert_fusion.12
  158.7 0.3 fusion.59
  159.0 1.7 convolution_multiply_fusion
  160.8 0.6 fusion.14
  161.7 0.3 reshape.239
  162.1 13.4 %psum.14 = f32[256,1]{0,1:T(1,128)S(1)} all-reduce(f32[256,1]{0,1:T(1,128)S(1)} %bitcast.96), channel_id=1, replica_groups=mesh['wide'=64,'narrow'=8] {'narrow'}, use_global_device_ids=true, to_apply=%region_3.4 | all-reduce | flops 256 | bytes 2048 | tf_op jit(solution)/shard_map/psum | solution.py:170
  175.6 2.4 convolution_convert_fusion.2
  178.1 1.7 convolution_convert_fusion.10
  179.7 0.7 convolution_convert_fusion.9
  180.5 68.5 %all-reduce.3.cloned.1.call-done = bf16[256,1536]{1,0:T(8,128)(2,1)} async-done(((bf16[256,1536]{1,0:T(8,128)(2,1)}), bf16[256,1536]{1,0:T(8,128)(2,1)}) %all-reduce.3.cloned.1.call-update) | async-done | bytes 786448 | tf_op jit(solution)/shard_map/psum | solution.py:175
  248.9 1.5 fusion.3
  250.5 0.7 copy.111
  251.3 1.3 convolution_convert_fusion.3
  252.6 3.7 %fusion.10 = bf16[2,8,192,128]{3,1,2,0:T(8,128)(2,1)S(1)} fusion(bf16[16,64]{1,0:T(8,128)(2,1)S(1)} %convolution_convert_fusion.12, bf16[8,8,192,128]{3,2,1,0:T(8,128)(2,1)} %bitcast.34), kind=kOutput, calls=%fused_computation.22 | convolution fusion | flops 50724864 | bytes 3934208 | tf_op jit(solution)/shard_map/dot_general | solution.py:224
  256.3 1.0 copy.124
  (107 shorter events, 4.1 us)
Async XLA Ops:
  7.2 244.1 %copy-start = (bf16[1536,403]{0,1:T(8,128)(2,1)S(1)}, bf16[1536,403]{0,1:T(8,128)(2,1)}, u32[]{:S(2)}) copy-start(bf16[1536,403]{0,1:T(8,128)(2,1)} %param.42) | copy-start | bytes 3714052
  7.2 7.0 %copy-start.1 = (s32[1024]{0:T(1024)S(1)}, s32[1024]{0:T(1024)}, u32[]{:S(2)}) copy-start(s32[1024]{0:T(1024)} %param.45) | copy-start | bytes 12292
  8.3 11.7 %collective-permute-start.1 = (bf16[256,192]{1,0:T(8,128)(2,1)S(1)}, bf16[256,192]{1,0:T(8,128)(2,1)S(1)}, u32[]{:S(2)}, u32[]{:S(2)}) collective-permute-start(bf16[256,192]{1,0:T(8,128)(2,1)S(1)} %copy.85), channel_id=1, source_target_pairs={{0,7},{1,0},{2,1},{3,2},{4,3},{5,4},{6,5},{7,6},{8,15},{9,8},{10,9... | collective-permute-start | bytes 294920 | tf_op jit(solution)/shard_map/ppermute | solution.py:27
  10.5 8.9 %collective-permute-start = (bf16[256,192]{1,0:T(8,128)(2,1)S(1)}, bf16[256,192]{1,0:T(8,128)(2,1)S(1)}, u32[]{:S(2)}, u32[]{:S(2)}) collective-permute-start(bf16[256,192]{1,0:T(8,128)(2,1)S(1)} %copy.85), channel_id=1, source_target_pairs={{0,1},{1,2},{2,3},{3,4},{4,5},{5,6},{6,7},{7,0},{8,9},{9,10},{10,1... | collective-permute-start | bytes 294920 | tf_op jit(solution)/shard_map/ppermute | solution.py:20
  14.2 4.6 %copy-start.12 = (s32[1024]{0:T(1024)S(1)}, s32[1024]{0:T(1024)}, u32[]{:S(2)}) copy-start(s32[1024]{0:T(1024)} %param.43) | copy-start | bytes 12292
  14.2 5.2 %copy-start.13 = (bf16[4,192]{1,0:T(4,128)(2,1)S(1)}, bf16[4,192]{1,0:T(4,128)(2,1)}, u32[]{:S(2)}) copy-start(bf16[4,192]{1,0:T(4,128)(2,1)} %param.34) | copy-start | bytes 4612
  14.2 5.2 %copy-start.14 = (bf16[4,256]{1,0:T(4,128)(2,1)S(1)}, bf16[4,256]{1,0:T(4,128)(2,1)}, u32[]{:S(2)}) copy-start(bf16[4,256]{1,0:T(4,128)(2,1)} %param.36) | copy-start | bytes 6148
  14.3 16.4 %copy-start.25 = (f32[3]{0:T(128)S(1)}, f32[3]{0:T(128)}, u32[]{:S(2)}) copy-start(f32[3]{0:T(128)} %param.33) | copy-start | bytes 40
  14.3 16.7 %copy-start.10 = (bf16[16,3,192]{2,0,1:T(8,128)(2,1)S(1)}, bf16[16,3,192]{2,0,1:T(8,128)(2,1)}, u32[]{:S(2)}) copy-start(bf16[16,3,192]{2,0,1:T(8,128)(2,1)} %param.26) | copy-start | bytes 55300
  14.3 16.7 %copy-start.11 = (bf16[16,3,256]{2,0,1:T(8,128)(2,1)S(1)}, bf16[16,3,256]{2,0,1:T(8,128)(2,1)}, u32[]{:S(2)}) copy-start(bf16[16,3,256]{2,0,1:T(8,128)(2,1)} %param.27) | copy-start | bytes 73732
  19.4 5.6 %collective-permute-start.2 = (bf16[256,192]{1,0:T(8,128)(2,1)S(1)}, bf16[256,192]{1,0:T(8,128)(2,1)S(1)}, u32[]{:S(2)}, u32[]{:S(2)}) collective-permute-start(bf16[256,192]{1,0:T(8,128)(2,1)S(1)} %collective-permute-done), channel_id=1, source_target_pairs={{0,1},{1,2},{2,3},{3,4},{4,5},{5,6},{6,7},{7,0},{8,9},{9,10},{10,1... | collective-permute-start | bytes 294920 | tf_op jit(solution)/shard_map/ppermute | solution.py:20
  20.0 5.5 %collective-permute-start.3 = (bf16[256,192]{1,0:T(8,128)(2,1)S(1)}, bf16[256,192]{1,0:T(8,128)(2,1)S(1)}, u32[]{:S(2)}, u32[]{:S(2)}) collective-permute-start(bf16[256,192]{1,0:T(8,128)(2,1)S(1)} %collective-permute-done.1), channel_id=1, source_target_pairs={{0,7},{1,0},{2,1},{3,2},{4,3},{5,4},{6,5},{7,6},{8,15},{9,8},{10,9... | collective-permute-start | bytes 294920 | tf_op jit(solution)/shard_map/ppermute | solution.py:27
  25.0 5.6 %collective-permute-start.4 = (bf16[256,192]{1,0:T(8,128)(2,1)S(1)}, bf16[256,192]{1,0:T(8,128)(2,1)S(1)}, u32[]{:S(2)}, u32[]{:S(2)}) collective-permute-start(bf16[256,192]{1,0:T(8,128)(2,1)S(1)} %collective-permute-done.2), channel_id=1, source_target_pairs={{0,1},{1,2},{2,3},{3,4},{4,5},{5,6},{6,7},{7,0},{8,9},{9,10},{10,1... | collective-permute-start | bytes 294920 | tf_op jit(solution)/shard_map/ppermute | solution.py:20
  25.5 12.9 %collective-permute-start.5 = (bf16[256,192]{1,0:T(8,128)(2,1)S(1)}, bf16[256,192]{1,0:T(8,128)(2,1)S(1)}, u32[]{:S(2)}, u32[]{:S(2)}) collective-permute-start(bf16[256,192]{1,0:T(8,128)(2,1)S(1)} %collective-permute-done.3), channel_id=1, source_target_pairs={{0,7},{1,0},{2,1},{3,2},{4,3},{5,4},{6,5},{7,6},{8,15},{9,8},{10,9... | collective-permute-start | bytes 294920 | tf_op jit(solution)/shard_map/ppermute | solution.py:27
  30.6 9.4 %collective-permute-start.6 = (bf16[256,192]{1,0:T(8,128)(2,1)S(1)}, bf16[256,192]{1,0:T(8,128)(2,1)S(1)}, u32[]{:S(2)}, u32[]{:S(2)}) collective-permute-start(bf16[256,192]{1,0:T(8,128)(2,1)S(1)} %collective-permute-done.4), channel_id=1, source_target_pairs={{0,1},{1,2},{2,3},{3,4},{4,5},{5,6},{6,7},{7,0},{8,9},{9,10},{10,1... | collective-permute-start | bytes 294920 | tf_op jit(solution)/shard_map/ppermute | solution.py:20
  30.9 30.2 %copy-start.15 = (s32[16]{0:T(128)}, s32[16]{0:T(128)S(1)}, u32[]{:S(2)}) copy-start(s32[16]{0:T(128)S(1)} %dynamic_slice.10) | copy-start | bytes 196
  31.1 10.3 %copy-start.21 = (bf16[1536,3]{0,1:T(4,128)(2,1)S(1)}, bf16[1536,3]{0,1:T(4,128)(2,1)}, u32[]{:S(2)}) copy-start(bf16[1536,3]{0,1:T(4,128)(2,1)} %param.31) | copy-start | bytes 27652
  31.1 10.3 %copy-start.22 = (f32[1536]{0:T(1024)S(1)}, f32[1536]{0:T(1024)}, u32[]{:S(2)}) copy-start(f32[1536]{0:T(1024)} %param.28) | copy-start | bytes 18436
  36.9 4.9 %copy-start.20 = (bf16[1536,32]{0,1:T(8,128)(2,1)S(1)}, bf16[1536,32]{0,1:T(8,128)(2,1)}, u32[]{:S(2)}) copy-start(bf16[1536,32]{0,1:T(8,128)(2,1)} %param.30) | copy-start | bytes 294916
  41.4 0.9 copy-start.19
  57.5 3.2 %copy-start.5 = (bf16[256,256]{1,0:T(8,128)(2,1)}, bf16[256,256]{1,0:T(8,128)(2,1)S(1)}, u32[]{:S(2)}) copy-start(bf16[256,256]{1,0:T(8,128)(2,1)S(1)} %copy.88) | copy-start | bytes 393220
  58.8 20.1 %copy-start.17 = (f32[192]{0:T(256)S(1)}, f32[192]{0:T(256)}, u32[]{:S(2)}) copy-start(f32[192]{0:T(256)} %param.35) | copy-start | bytes 2308
  60.7 1.4 copy-start.8
  62.1 28.9 %all-to-all-start.1 = ((bf16[64,3,192]{2,1,0:T(4,128)(2,1)}), bf16[64,3,192]{2,1,0:T(4,128)(2,1)}, u32[]{:S(2)}, u32[]{:S(2)}) async-start(bf16[64,3,192]{2,1,0:T(4,128)(2,1)} %copy.106), calls=%async_computation.1 | async-start | bytes 262144 | tf_op jit(solution)/shard_map/all_to_all | solution.py:209
  78.9 18.5 %copy-start.2 = (bf16[16,3,64,128]{3,2,1,0:T(8,128)(2,1)S(1)}, bf16[16,3,64,128]{3,2,1,0:T(8,128)(2,1)}, u32[]{:S(2)}) copy-start(bf16[16,3,64,128]{3,2,1,0:T(8,128)(2,1)} %param.25) | copy-start | bytes 2359300
  81.0 2.2 copy-start.3
  91.1 18.1 %all-to-all-start.2 = ((bf16[64,3,256]{2,1,0:T(4,128)(2,1)}), bf16[64,3,256]{2,1,0:T(4,128)(2,1)S(1)}, u32[]{:S(2)}, u32[]{:S(2)}) async-start(bf16[64,3,256]{2,1,0:T(4,128)(2,1)} %copy.109), calls=%async_computation.2 | async-start | bytes 262144 | tf_op jit(solution)/shard_map/all_to_all | solution.py:210
  109.1 0.6 copy-start.6
  109.8 142.8 %all-to-all-start = ((bf16[64,3,64,128]{3,2,1,0:T(8,128)(2,1)}), bf16[64,3,64,128]{3,2,1,0:T(8,128)(2,1)}, u32[]{:S(2)}, u32[]{:S(2)}) async-start(bf16[64,3,64,128]{3,2,1,0:T(8,128)(2,1)} %bitcast.87), calls=%async_computation | async-start | bytes 6291456 | tf_op jit(solution)/shard_map/all_to_all | solution.py:208
  119.0 129.9 %all-reduce.3.cloned.1.call-start = ((), (), s32[]{:S(2)}) async-start(), calls=%async_computation.3 | async-start | bytes 1572864 | tf_op jit(solution)/shard_map/psum | solution.py:175
  152.9 4.6 %copy-start.16 = (pred[1024]{0:T(1024)(128)(4,1)S(1)}, pred[1024]{0:T(1024)(128)(4,1)}, u32[]{:S(2)}) copy-start(pred[1024]{0:T(1024)(128)(4,1)} %get-tuple-element.28) | copy-start | bytes 3076
  152.9 4.6 %copy-start.18 = (pred[1024]{0:T(1024)(128)(4,1)S(1)}, pred[1024]{0:T(1024)(128)(4,1)}, u32[]{:S(2)}) copy-start(pred[1024]{0:T(1024)(128)(4,1)} %get-tuple-element.26) | copy-start | bytes 3076
  157.4 3.3 %copy-start.26 = (f32[3]{0:T(128)S(1)}, f32[3]{0:T(128)}, u32[]{:S(2)}) copy-start(f32[3]{0:T(128)} %param.38) | copy-start | bytes 40
  158.7 2.1 copy-start.4
  160.8 1.2 copy-start.9
  160.8 14.8 %copy-start.24 = (f32[192]{0:T(256)S(1)}, f32[192]{0:T(256)}, u32[]{:S(2)}) copy-start(f32[192]{0:T(256)} %param.39) | copy-start | bytes 2308
  175.6 4.1 %copy-start.7 = (bf16[64,3,256]{2,1,0:T(4,128)(2,1)S(1)}, bf16[64,3,256]{2,1,0:T(4,128)(2,1)}, u32[]{:S(2)}) copy-start(bf16[64,3,256]{2,1,0:T(4,128)(2,1)} %copy-done.6) | copy-start | bytes 294916
  178.0 73.2 %copy-start.23 = (f32[1536]{0:T(1024)S(1)}, f32[1536]{0:T(1024)}, u32[]{:S(2)}) copy-start(f32[1536]{0:T(1024)} %param.41) | copy-start | bytes 18436
Sparse Core Ops, SparseCore 0:
  178.2 70.7 all-reduce.2
